TPU v7x, 32 devices: a whole 2x2x4 slice. The times are simulated.
32 devices in a mesh: blk: 16 (over z, y, x), grp: 2 (over core).
Axes of the slice: x: 2, y: 2, z: 4, core: 2. Of those that a mesh axis runs over, the one named last changes fastest.
Arguments:
- schur_blocks: bfloat16 [64, 1024, 1024], P(('blk', 'grp')), may hold values from -1 to 5, as said below
- residual: float32 [64, 1024, 128], P(('blk', 'grp')), may hold values from -200 to 200
- direction: float32 [64, 1024, 128], P(('blk', 'grp')), may hold values from -200 to 200
- corner_map: int32 [64, 24], P(('blk', 'grp')), may hold values from 0 to 511
- panel_order: int32 [8], replicated, may hold values from 0 to 7, each once
- coarse_factor: float32 [8, 8, 1024, 1024], P(None, None, 'blk'), may hold values from -0.0625 to 0.0625
- block_inverses: float32 [8, 1024, 1024], P(None, 'blk'), may hold values from -0.1875 to 0.1875
Outputs:
- residual_next: float32 [64, 1024, 128], P(('blk', 'grp'))
- direction_next: float32 [64, 1024, 128], P(('blk', 'grp'))
Inputs may be any that keep to these rules, and one draw needn't show every extreme that they name: `schur_blocks`: each subdomain's block is symmetric positive definite. `panel_order`: each coarse block appears once.
All inputs are finite; a program needn't handle non-finite values.
Results may differ from a plain program's by a relative error of at most 0.0048.
Values sent between devices are 32-bit elements; how exact they have to be, the bound alone decides.
No kernel may reach another device: no remote copies, remote signals or barrier semaphores. Data moves between devices by JAX's collectives and lax.ppermute only.
A program may use at most 64 MiB of HBM per device.

v0:
```python
import jax
import jax.numpy as jnp
from jax import lax
from jax.sharding import PartitionSpec as P

PANELS = 8
precise = lax.Precision.HIGHEST


def squares(residual):
    return lax.psum(jnp.sum(residual * residual, axis=(0, 1)), ("blk", "grp"))


def solve(coarse, panel_order, coarse_factor, block_inverses):
    pending = jnp.zeros_like(coarse)
    solved = jnp.zeros_like(coarse)
    for position in range(PANELS):
        current = panel_order[position]
        target = lax.dynamic_index_in_dim(coarse - pending, current, 0, keepdims=False)
        inverse = lax.dynamic_index_in_dim(block_inverses, current, 0, keepdims=False)
        block_value = jnp.dot(
            inverse,
            lax.all_gather(target, "blk", axis=0, tiled=True),
            precision=precise,
            preferred_element_type=jnp.float32,
        )
        solved = lax.dynamic_update_index_in_dim(solved, block_value, current, 0)
        if position + 1 < PANELS:
            coupling = lax.dynamic_index_in_dim(coarse_factor, current, 1, keepdims=False)
            pending = pending + jnp.einsum(
                "aic,cv->aiv",
                coupling,
                lax.all_gather(block_value, "blk", axis=0, tiled=True),
                precision=precise,
            )
    return solved


def local(
    schur_blocks, residual, direction, corner_map, panel_order, coarse_factor, block_inverses
):
    panels = block_inverses.shape[0]
    rows_b = block_inverses.shape[1]
    sub_count = schur_blocks.shape[0]
    corners = corner_map.shape[1]
    columns_iota = lax.broadcasted_iota(jnp.int32, (sub_count, corners, panels * rows_b), 2)
    placing = (corner_map[:, :, None] == columns_iota).astype(jnp.float32)
    norm_now = squares(residual)
    applied = jnp.einsum(
        "sij,sjv->siv",
        schur_blocks,
        direction.astype(jnp.bfloat16),
        preferred_element_type=jnp.float32,
    )
    curvature = lax.psum(jnp.sum(direction * applied, axis=(0, 1)), ("blk", "grp"))
    step_size = norm_now / curvature
    residual = residual - step_size * applied
    norm_next = squares(residual)
    corner_part = jnp.einsum("scm,scv->mv", placing, residual[:, :corners, :], precision=precise)
    corner_part = corner_part.reshape(panels, rows_b, -1)
    coarse_part = lax.psum(corner_part, "grp")
    solved = solve(coarse_part, panel_order, coarse_factor, block_inverses)
    flat_solved = solved.reshape(panels * rows_b, -1)
    correction = jnp.einsum("scm,mv->scv", placing, flat_solved, precision=precise)
    corrected = jnp.concatenate(
        [residual[:, :corners, :] + correction, residual[:, corners:, :]], axis=1
    )
    direction = corrected + norm_next / norm_now * direction
    return (residual, direction)


def solution(mesh):
    in_specs = (
        P(("blk", "grp"), None, None),
        P(("blk", "grp"), None, None),
        P(("blk", "grp"), None, None),
        P(("blk", "grp"), None),
        P(),
        P(None, None, "blk", None),
        P(None, "blk", None),
    )
    out_specs = (P(("blk", "grp"), None, None), P(("blk", "grp"), None, None))
    return jax.shard_map(local, mesh=mesh, in_specs=in_specs, out_specs=out_specs, check_vma=False)
```

profile of v0, /device:TPU:0, one launch (start us, length us, event | category | flops | bytes accessed | tf_op | source)
XLA Modules:
  0.0 743.4 jit_solution(7819238958384494164)
XLA Ops:
  7.2 0.0 copy-start
  7.2 0.0 all-reduce.3.cloned.1.call-start
  7.2 1.6 multiply_reduce_fusion.2
  8.9 5.0 multiply_reduce_fusion.1
  13.9 41.9 %all-reduce = (f32[128]{0:T(128)S(1)}, f32[128]{0:T(128)S(1)}) all-reduce(f32[128]{0:T(128)S(1)} %multiply_reduce_fusion.2, f32[128]{0:T(128)S(1)} %get-tuple-element.14), channel_id=1, replica_groups=mesh['blk'=16,'grp'=2] {'blk','grp'}, use_global_device_ids=true, to_apply=%region_1.0 | all-reduce | flops 256 | bytes 2048 | tf_op jit(solution)/shard_map/psum | solution.py:11
  55.8 1.8 multiply_reduce_fusion
  57.7 0.0 copy-done.7
  57.7 1.2 fusion.77
  58.8 0.0 all-reduce.3.cloned.1.call-update
  58.9 0.7 fusion.96
  69.5 1.0 slice.42
  70.6 40.0 %psum.31 = f32[128]{0:T(128)S(1)} all-reduce(f32[128]{0:T(128)S(1)} %get-tuple-element.4), channel_id=1, replica_groups=mesh['blk'=16,'grp'=2] {'blk','grp'}, use_global_device_ids=true, to_apply=%region_6.0 | all-reduce | flops 128 | bytes 1024 | tf_op jit(solution)/shard_map/psum | solution.py:11
  115.6 0.0 all-reduce.3.cloned.1.call-done
  115.7 0.8 constant_dynamic-slice_fusion
  116.4 43.7 %all-gather = f32[1,1024,128]{2,1,0:T(8,128)S(1)} all-gather(f32[1,64,128]{2,1,0:T(8,128)S(1)} %constant_dynamic-slice_fusion), channel_id=2, replica_groups=mesh['blk'=16,'grp'=2] {'blk'}, dimensions={1}, use_global_device_ids=true | all-gather | bytes 557056 | tf_op jit(solution)/shard_map/all_gather | solution.py:23
  160.2 0.0 copy-start.1
  160.2 0.5 bitcast_dynamic-update-slice_fusion.6
  160.7 38.5 %all_gather.46 = f32[1024,128]{1,0:T(8,128)S(1)} all-gather(f32[64,128]{1,0:T(8,128)S(1)} %get-tuple-element.17), channel_id=1, replica_groups=mesh['blk'=16,'grp'=2] {'blk'}, dimensions={0}, use_global_device_ids=true | all-gather | bytes 557056 | tf_op jit(solution)/shard_map/all_gather | solution.py:33
  199.2 3.4 fusion.12
  202.6 0.0 copy-done.5
  202.6 40.7 %all-gather.1 = f32[1,1024,128]{2,1,0:T(8,128)S(1)} all-gather(f32[1,64,128]{2,1,0:T(8,128)S(1)} %dynamic-slice_subtract_fusion.6), channel_id=3, replica_groups=mesh['blk'=16,'grp'=2] {'blk'}, dimensions={1}, use_global_device_ids=true | all-gather | bytes 557056 | tf_op jit(solution)/shard_map/all_gather | solution.py:23
  243.3 0.5 bitcast_dynamic-update-slice_fusion.5
  243.8 38.6 %all_gather.48 = f32[1024,128]{1,0:T(8,128)S(1)} all-gather(f32[64,128]{1,0:T(8,128)S(1)} %get-tuple-element.19), channel_id=1, replica_groups=mesh['blk'=16,'grp'=2] {'blk'}, dimensions={0}, use_global_device_ids=true | all-gather | bytes 557056 | tf_op jit(solution)/shard_map/all_gather | solution.py:33
  282.4 3.4 fusion.21
  285.8 40.3 %all-gather.2 = f32[1,1024,128]{2,1,0:T(8,128)S(1)} all-gather(f32[1,64,128]{2,1,0:T(8,128)S(1)} %dynamic-slice_subtract_fusion.5), channel_id=4, replica_groups=mesh['blk'=16,'grp'=2] {'blk'}, dimensions={1}, use_global_device_ids=true | all-gather | bytes 557056 | tf_op jit(solution)/shard_map/all_gather | solution.py:23
  326.1 0.5 bitcast_dynamic-update-slice_fusion.4
  326.6 38.6 %all_gather.50 = f32[1024,128]{1,0:T(8,128)S(1)} all-gather(f32[64,128]{1,0:T(8,128)S(1)} %get-tuple-element.21), channel_id=1, replica_groups=mesh['blk'=16,'grp'=2] {'blk'}, dimensions={0}, use_global_device_ids=true | all-gather | bytes 557056 | tf_op jit(solution)/shard_map/all_gather | solution.py:33
  365.2 3.4 fusion.24
  368.6 41.1 %all-gather.3 = f32[1,1024,128]{2,1,0:T(8,128)S(1)} all-gather(f32[1,64,128]{2,1,0:T(8,128)S(1)} %dynamic-slice_subtract_fusion.4), channel_id=5, replica_groups=mesh['blk'=16,'grp'=2] {'blk'}, dimensions={1}, use_global_device_ids=true | all-gather | bytes 557056 | tf_op jit(solution)/shard_map/all_gather | solution.py:23
  409.8 0.5 bitcast_dynamic-update-slice_fusion.3
  410.2 38.3 %all_gather.52 = f32[1024,128]{1,0:T(8,128)S(1)} all-gather(f32[64,128]{1,0:T(8,128)S(1)} %get-tuple-element.23), channel_id=1, replica_groups=mesh['blk'=16,'grp'=2] {'blk'}, dimensions={0}, use_global_device_ids=true | all-gather | bytes 557056 | tf_op jit(solution)/shard_map/all_gather | solution.py:33
  448.5 1.8 fusion.27
  450.3 40.8 %all-gather.4 = f32[1,1024,128]{2,1,0:T(8,128)S(1)} all-gather(f32[1,64,128]{2,1,0:T(8,128)S(1)} %dynamic-slice_subtract_fusion.3), channel_id=6, replica_groups=mesh['blk'=16,'grp'=2] {'blk'}, dimensions={1}, use_global_device_ids=true | all-gather | bytes 557056 | tf_op jit(solution)/shard_map/all_gather | solution.py:23
  491.1 0.5 bitcast_dynamic-update-slice_fusion.2
  491.6 38.6 %all_gather.54 = f32[1024,128]{1,0:T(8,128)S(1)} all-gather(f32[64,128]{1,0:T(8,128)S(1)} %get-tuple-element.25), channel_id=1, replica_groups=mesh['blk'=16,'grp'=2] {'blk'}, dimensions={0}, use_global_device_ids=true | all-gather | bytes 557056 | tf_op jit(solution)/shard_map/all_gather | solution.py:33
  530.2 1.8 fusion.30
  532.0 40.5 %all-gather.5 = f32[1,1024,128]{2,1,0:T(8,128)S(1)} all-gather(f32[1,64,128]{2,1,0:T(8,128)S(1)} %dynamic-slice_subtract_fusion.2), channel_id=7, replica_groups=mesh['blk'=16,'grp'=2] {'blk'}, dimensions={1}, use_global_device_ids=true | all-gather | bytes 557056 | tf_op jit(solution)/shard_map/all_gather | solution.py:23
  572.5 0.4 bitcast_dynamic-update-slice_fusion.1
  573.0 38.5 %all_gather.56 = f32[1024,128]{1,0:T(8,128)S(1)} all-gather(f32[64,128]{1,0:T(8,128)S(1)} %get-tuple-element.27), channel_id=1, replica_groups=mesh['blk'=16,'grp'=2] {'blk'}, dimensions={0}, use_global_device_ids=true | all-gather | bytes 557056 | tf_op jit(solution)/shard_map/all_gather | solution.py:33
  611.4 1.8 fusion.33
  613.3 40.4 %all-gather.6 = f32[1,1024,128]{2,1,0:T(8,128)S(1)} all-gather(f32[1,64,128]{2,1,0:T(8,128)S(1)} %dynamic-slice_subtract_fusion.1), channel_id=8, replica_groups=mesh['blk'=16,'grp'=2] {'blk'}, dimensions={1}, use_global_device_ids=true | all-gather | bytes 557056 | tf_op jit(solution)/shard_map/all_gather | solution.py:23
  653.6 0.5 bitcast_dynamic-update-slice_fusion
  654.1 38.3 %all_gather.58 = f32[1024,128]{1,0:T(8,128)S(1)} all-gather(f32[64,128]{1,0:T(8,128)S(1)} %get-tuple-element.29), channel_id=1, replica_groups=mesh['blk'=16,'grp'=2] {'blk'}, dimensions={0}, use_global_device_ids=true | all-gather | bytes 557056 | tf_op jit(solution)/shard_map/all_gather | solution.py:33
  692.4 1.8 fusion
  694.2 40.5 %all-gather.7 = f32[1,1024,128]{2,1,0:T(8,128)S(1)} all-gather(f32[1,64,128]{2,1,0:T(8,128)S(1)} %dynamic-slice_subtract_fusion), channel_id=9, replica_groups=mesh['blk'=16,'grp'=2] {'blk'}, dimensions={1}, use_global_device_ids=true | all-gather | bytes 557056 | tf_op jit(solution)/shard_map/all_gather | solution.py:23
  734.7 0.5 fusion.36
  735.2 0.2 convolution_add_fusion
  735.4 1.1 maximum_add_fusion
  (22 shorter events, 0.1 us)
Async XLA Ops:
  7.2 153.0 %copy-start = (f32[8,64,1024]{2,1,0:T(8,128)S(1)}, f32[8,64,1024]{2,1,0:T(8,128)}, u32[]{:S(2)}) copy-start(f32[8,64,1024]{2,1,0:T(8,128)} %param.13) | copy-start | bytes 6291460
  7.2 108.5 %all-reduce.3.cloned.1.call-start = ((), (), s32[]{:S(2)}) async-start(), calls=%async_computation | async-start | bytes 524288 | tf_op jit(solution)/shard_map/psum | solution.py:61
  13.9 43.8 %copy-start.7 = (s32[2,24]{1,0:T(2,128)S(1)}, s32[2,24]{1,0:T(2,128)}, u32[]{:S(2)}) copy-start(s32[2,24]{1,0:T(2,128)} %param.10) | copy-start | bytes 580
  13.9 45.0 %copy-start.6 = (s32[8]{0:T(128)S(1)}, s32[8]{0:T(128)}, u32[]{:S(2)}) copy-start(s32[8]{0:T(128)} %param.11) | copy-start | bytes 100
  57.6 677.5 %copy-start.2 = (f32[2,1024,128]{2,1,0:T(8,128)}, f32[2,1024,128]{2,1,0:T(8,128)S(1)}, u32[]{:S(2)}) copy-start(f32[2,1024,128]{2,1,0:T(8,128)S(1)} %get-tuple-element.5) | copy-start | bytes 3145732
  160.2 42.4 %copy-start.5 = (f32[8,64,128]{2,1,0:T(8,128)S(1)}, f32[8,64,128]{2,1,0:T(8,128)}, u32[]{:S(2)}) copy-start(f32[8,64,128]{2,1,0:T(8,128)} %all-reduce.3.cloned.1.call-done) | copy-start | bytes 786436
  160.2 288.3 %copy-start.1 = (f32[8,8,64,1024]{3,2,1,0:T(8,128)S(1)}, f32[8,8,64,1024]{3,2,1,0:T(8,128)}, u32[]{:S(2)}) copy-start(f32[8,8,64,1024]{3,2,1,0:T(8,128)} %param.12) | copy-start | bytes 50331652
  692.4 43.1 %copy-start.3 = (f32[2,1024,128]{2,1,0:T(8,128)S(1)}, f32[2,1024,128]{2,1,0:T(8,128)}, u32[]{:S(2)}) copy-start(f32[2,1024,128]{2,1,0:T(8,128)} %param.9) | copy-start | bytes 3145732
  692.4 43.1 %copy-start.4 = (f32[2,1000,128]{2,1,0:T(8,128)S(1)}, f32[2,1000,128]{2,1,0:T(8,128)}, u32[]{:S(2)}) copy-start(f32[2,1000,128]{2,1,0:T(8,128)} %slice.42) | copy-start | bytes 3072004
Sparse Core Ops, SparseCore 0:
  59.0 18.0 all-reduce.2
where the time goes:
time: 744 us; the launch traced here: 743 us
  blocking collectives  679 us (91%)
  between operations  29.3 us (4%)
  matrix products  27.4 us (4%)
    all_gather x8, blocking collectives, solve(): lax.all_gather(target, 'blk', axis=0, tiled=True)  328 us
    all_gather x7, blocking collectives, solve(): lax.all_gather(block_value, 'blk', axis=0, tiled=True)  269 us
    psum x2, blocking collectives, squares(): return lax.psum(jnp.sum(residual * residual, axis=(0, 1)), ('blk', 'grp'))  82 us
    dot_general x7, matrix products, solve(): jnp.einsum('aic,cv->aiv', coupling, lax.all_gather(block_value, 'blk', ax...  17.4 us
  transfers between devices with their start and end apart: 1, of which 0 were waited for; matrix products, arithmetic and copies ran while one was open for 0% of the time, Pallas kernels for 0%

commit v1 on v0

--- a/solution.py
+++ b/solution.py
@@ -2,6 +2,7 @@
 import jax.numpy as jnp
 from jax import lax
 from jax.sharding import PartitionSpec as P
+from jax.lax import axis_index, ppermute, psum
 
 PANELS = 8
 precise = lax.Precision.HIGHEST
@@ -27,11 +28,37 @@
         solved = lax.dynamic_update_index_in_dim(solved, block_value, current, 0)
         if position + 1 < PANELS:
             coupling = lax.dynamic_index_in_dim(coarse_factor, current, 1, keepdims=False)
-            pending = pending + jnp.einsum(
-                "aic,cv->aiv",
-                coupling,
-                lax.all_gather(block_value, "blk", axis=0, tiled=True),
-                precision=precise,
+
+            def review_forms(array_in, w_in):
+                mesh_dim = "blk"
+                reached, current_value, b_now = (
+                    psum(1, mesh_dim),
+                    axis_index(mesh_dim),
+                    array_in.shape[0],
+                )
+                entries = tuple(((dev_j, (dev_j + 1) % reached) for dev_j in range(reached)))
+                sheets = tuple(((dev_j, (dev_j - 1) % reached) for dev_j in range(reached)))
+                reply = reached // 2
+                odd = z1 = array_in
+                all_values = w_in(array_in, current_value * b_now)
+                for hop_no in range(1, reply + 1):
+                    odd = ppermute(odd, mesh_dim, entries)
+                    if hop_no < reached - reply:
+                        z1 = ppermute(z1, mesh_dim, sheets)
+                        all_values = all_values + w_in(
+                            z1, (current_value + hop_no) % reached * b_now
+                        )
+                    all_values = all_values + w_in(odd, (current_value - hop_no) % reached * b_now)
+                return all_values
+
+            pending = pending + review_forms(
+                block_value,
+                lambda part, start: jnp.einsum(
+                    "aic,cv->aiv",
+                    lax.dynamic_slice_in_dim(coupling, start, part.shape[0], axis=2),
+                    part,
+                    precision=precise,
+                ),
             )
     return solved
 

time: 744 us -> 929 us (1.25)
  blocking collectives: 679 us -> 397 us
  starting transfers between devices: 0.04 us -> 254 us
  waiting for transfers between devices: 0.04 us -> 152 us
  matrix products: 27.4 us -> 77.5 us
    all_gather x7 -> x0, blocking collectives: 269 us -> none  [solve(): lax.all_gather(block_value, 'blk', axis=0, tiled=True)]
    ppermute x0 -> x105, starting transfers between devices: none -> 254 us  [the longest x49 246 us: review_forms(): z1 = ppermute(z1, mesh_dim, sheets)]
    ppermute x0 -> x105, waiting for transfers between devices: none -> 152 us  [the longest x56 143 us: review_forms(): odd = ppermute(odd, mesh_dim, entries)]
    dot_general x7 -> x112, matrix products: 17.4 us -> 66.8 us  [solve(): jnp.einsum('aic,cv->aiv', lax.dynamic_slice_in_dim(coupling, start, part....]
    all_gather x8, blocking collectives: 328 us -> 314 us  [solve(): lax.all_gather(target, 'blk', axis=0, tiled=True)]
  transfers between devices with their start and end apart: 1 -> 106, of which waited for: 0 -> 50; matrix products, arithmetic and copies ran while one was open for 0% -> 7% of each run, Pallas kernels for 0% -> 0%
where the time goes in v1:
time: 929 us; the launch traced here: 920 us
  blocking collectives  397 us (43%)
  starting transfers between devices  254 us (27%)
  waiting for transfers between devices  152 us (16%)
  matrix products  77.5 us (8%)
  between operations  31.2 us (3%)
    all_gather x8, blocking collectives, solve(): lax.all_gather(target, 'blk', axis=0, tiled=True)  314 us
    ppermute x49, starting transfers between devices, review_forms(): z1 = ppermute(z1, mesh_dim, sheets)  246 us
    ppermute x56, waiting for transfers between devices, review_forms(): odd = ppermute(odd, mesh_dim, entries)  143 us
    psum x2, blocking collectives, squares(): return lax.psum(jnp.sum(residual * residual, axis=(0, 1)), ('blk', 'grp'))  82 us
    dot_general x112, matrix products, solve(): jnp.einsum('aic,cv->aiv', lax.dynamic_slice_in_dim(coupling, start, part....  66.8 us
  transfers between devices with their start and end apart: 106, of which 50 were waited for; matrix products, arithmetic and copies ran while one was open for 7% of the time, Pallas kernels for 0%

profile of v1, /device:TPU:0, one launch (start us, length us, event | category | flops | bytes accessed | tf_op | source)
XLA Modules:
  0.0 919.6 jit_solution(7226736238444284259)
XLA Ops:
  13.9 41.9 %all-reduce = (f32[128]{0:T(128)S(1)}, f32[128]{0:T(128)S(1)}) all-reduce(f32[128]{0:T(128)S(1)} %multiply_reduce_fusion.2, f32[128]{0:T(128)S(1)} %get-tuple-element.14), channel_id=1, replica_groups=mesh['blk'=16,'grp'=2] {'blk','grp'}, use_global_device_ids=true, to_apply=%region_1.0 | all-reduce | flops 256 | bytes 2048 | tf_op jit(solution)/shard_map/psum | solution.py:12
  76.7 40.1 %psum.31 = f32[128]{0:T(128)S(1)} all-reduce(f32[128]{0:T(128)S(1)} %get-tuple-element.4), channel_id=1, replica_groups=mesh['blk'=16,'grp'=2] {'blk','grp'}, use_global_device_ids=true, to_apply=%region_6.0 | all-reduce | flops 128 | bytes 1024 | tf_op jit(solution)/shard_map/psum | solution.py:12
  118.4 43.9 %all-gather = f32[1,1024,128]{2,1,0:T(8,128)S(1)} all-gather(f32[1,64,128]{2,1,0:T(8,128)S(1)} %constant_dynamic-slice_fusion.19), channel_id=2, replica_groups=mesh['blk'=16,'grp'=2] {'blk'}, dimensions={1}, use_global_device_ids=true | all-gather | bytes 557056 | tf_op jit(solution)/shard_map/all_gather | solution.py:24
  170.4 5.6 collective-permute-start.2
  180.4 5.7 collective-permute-start.4
  189.2 5.6 collective-permute-start.6
  197.9 5.6 collective-permute-start.8
  206.6 5.6 collective-permute-start.10
  215.3 5.6 collective-permute-start.12
  232.4 39.9 %all-gather.1 = f32[1,1024,128]{2,1,0:T(8,128)S(1)} all-gather(f32[1,64,128]{2,1,0:T(8,128)S(1)} %fusion.477), channel_id=3, replica_groups=mesh['blk'=16,'grp'=2] {'blk'}, dimensions={1}, use_global_device_ids=true | all-gather | bytes 557056 | tf_op jit(solution)/shard_map/all_gather | solution.py:24
  283.0 7.1 collective-permute-done.18
  290.7 5.6 collective-permute-start.19
  298.7 5.6 collective-permute-start.21
  306.7 5.6 collective-permute-start.23
  314.8 5.6 collective-permute-start.25
  323.1 5.6 collective-permute-start.27
  331.8 7.4 collective-permute-done.29
  339.7 38.5 %all-gather.2 = f32[1,1024,128]{2,1,0:T(8,128)S(1)} all-gather(f32[1,64,128]{2,1,0:T(8,128)S(1)} %fusion.478), channel_id=4, replica_groups=mesh['blk'=16,'grp'=2] {'blk'}, dimensions={1}, use_global_device_ids=true | all-gather | bytes 557056 | tf_op jit(solution)/shard_map/all_gather | solution.py:24
  382.8 5.9 collective-permute-start.32
  389.6 7.4 collective-permute-done.33
  397.5 5.8 collective-permute-start.34
  413.5 5.6 collective-permute-start.38
  421.5 5.6 collective-permute-start.40
  429.9 5.6 collective-permute-start.42
  438.3 7.0 collective-permute-done.44
  445.8 38.6 %all-gather.3 = f32[1,1024,128]{2,1,0:T(8,128)S(1)} all-gather(f32[1,64,128]{2,1,0:T(8,128)S(1)} %fusion.479), channel_id=5, replica_groups=mesh['blk'=16,'grp'=2] {'blk'}, dimensions={1}, use_global_device_ids=true | all-gather | bytes 557056 | tf_op jit(solution)/shard_map/all_gather | solution.py:24
  488.8 5.8 collective-permute-start.47
  495.6 7.3 collective-permute-done.48
  503.4 5.6 collective-permute-start.49
  511.4 5.6 collective-permute-start.51
  519.6 5.6 collective-permute-start.53
  527.6 5.6 collective-permute-start.55
  535.6 5.6 collective-permute-start.57
  544.5 7.0 collective-permute-done.59
  552.0 38.5 %all-gather.4 = f32[1,1024,128]{2,1,0:T(8,128)S(1)} all-gather(f32[1,64,128]{2,1,0:T(8,128)S(1)} %fusion.480), channel_id=6, replica_groups=mesh['blk'=16,'grp'=2] {'blk'}, dimensions={1}, use_global_device_ids=true | all-gather | bytes 557056 | tf_op jit(solution)/shard_map/all_gather | solution.py:24
  595.0 5.7 collective-permute-start.62
  601.6 7.2 collective-permute-done.63
  649.9 7.0 collective-permute-done.74
  657.4 38.4 %all-gather.5 = f32[1,1024,128]{2,1,0:T(8,128)S(1)} all-gather(f32[1,64,128]{2,1,0:T(8,128)S(1)} %fusion.481), channel_id=7, replica_groups=mesh['blk'=16,'grp'=2] {'blk'}, dimensions={1}, use_global_device_ids=true | all-gather | bytes 557056 | tf_op jit(solution)/shard_map/all_gather | solution.py:24
  706.7 7.1 collective-permute-done.78
  722.3 5.8 collective-permute-start.81
  754.8 7.0 collective-permute-done.89
  762.3 38.5 %all-gather.6 = f32[1,1024,128]{2,1,0:T(8,128)S(1)} all-gather(f32[1,64,128]{2,1,0:T(8,128)S(1)} %fusion.482), channel_id=8, replica_groups=mesh['blk'=16,'grp'=2] {'blk'}, dimensions={1}, use_global_device_ids=true | all-gather | bytes 557056 | tf_op jit(solution)/shard_map/all_gather | solution.py:24
  811.7 7.2 collective-permute-done.93
  850.6 5.9 collective-permute-start.102
  857.5 7.1 collective-permute-done.103
  865.4 6.6 collective-permute-done.104
  872.5 38.3 %all-gather.7 = f32[1,1024,128]{2,1,0:T(8,128)S(1)} all-gather(f32[1,64,128]{2,1,0:T(8,128)S(1)} %fusion.484), channel_id=9, replica_groups=mesh['blk'=16,'grp'=2] {'blk'}, dimensions={1}, use_global_device_ids=true | all-gather | bytes 557056 | tf_op jit(solution)/shard_map/all_gather | solution.py:24
  (328 shorter events, 257.8 us)
Async XLA Ops:
  7.2 110.3 %all-reduce.3.cloned.1.call-start = ((), (), s32[]{:S(2)}) async-start(), calls=%async_computation | async-start | bytes 524288 | tf_op jit(solution)/shard_map/psum | solution.py:88
  170.4 8.5 collective-permute-start.3
  170.4 10.0 %collective-permute-start.2 = (f32[64,128]{1,0:T(8,128)S(1)}, f32[64,128]{1,0:T(8,128)S(1)}, u32[]{:S(2)}, u32[]{:S(2)}) collective-permute-start(f32[64,128]{1,0:T(8,128)S(1)} %collective-permute-done), channel_id=1, source_target_pairs={{0,30},{2,0},{4,2},{6,4},{8,6},{10,8},{12,10},{14,12},{16,14},{18,... | collective-permute-start | bytes 98312 | tf_op jit(solution)/shard_map/ppermute | solution.py:47
  178.9 8.7 collective-permute-start.5
  180.4 8.8 collective-permute-start.4
  187.6 8.7 collective-permute-start.7
  189.2 8.7 collective-permute-start.6
  196.3 8.7 collective-permute-start.9
  197.9 8.7 collective-permute-start.8
  205.0 8.7 collective-permute-start.11
  206.6 8.7 collective-permute-start.10
  213.7 8.7 collective-permute-start.13
  215.3 8.9 collective-permute-start.12
  273.5 9.0 collective-permute-start.16
  276.8 13.9 %collective-permute-start.17 = (f32[64,128]{1,0:T(8,128)S(1)}, f32[64,128]{1,0:T(8,128)S(1)}, u32[]{:S(2)}, u32[]{:S(2)}) collective-permute-start(f32[64,128]{1,0:T(8,128)S(1)} %collective-permute-done.15), channel_id=1, source_target_pairs={{0,30},{2,0},{4,2},{6,4},{8,6},{10,8},{12,10},{14,12},{16,14},{18,... | collective-permute-start | bytes 98312 | tf_op jit(solution)/shard_map/ppermute | solution.py:47
  298.7 8.0 collective-permute-start.21
  306.7 8.1 collective-permute-start.23
  314.8 8.3 collective-permute-start.25
  323.1 8.3 collective-permute-start.27
  380.9 8.2 collective-permute-start.31
  382.8 14.7 %collective-permute-start.32 = (f32[64,128]{1,0:T(8,128)S(1)}, f32[64,128]{1,0:T(8,128)S(1)}, u32[]{:S(2)}, u32[]{:S(2)}) collective-permute-start(f32[64,128]{1,0:T(8,128)S(1)} %collective-permute-done.30), channel_id=1, source_target_pairs={{0,30},{2,0},{4,2},{6,4},{8,6},{10,8},{12,10},{14,12},{16,14},{18,... | collective-permute-start | bytes 98312 | tf_op jit(solution)/shard_map/ppermute | solution.py:47
  405.5 8.0 collective-permute-start.36
  413.5 8.1 collective-permute-start.38
  421.5 8.3 collective-permute-start.40
  429.9 8.0 collective-permute-start.42
  486.8 8.2 collective-permute-start.46
  488.8 14.5 %collective-permute-start.47 = (f32[64,128]{1,0:T(8,128)S(1)}, f32[64,128]{1,0:T(8,128)S(1)}, u32[]{:S(2)}, u32[]{:S(2)}) collective-permute-start(f32[64,128]{1,0:T(8,128)S(1)} %collective-permute-done.45), channel_id=1, source_target_pairs={{0,30},{2,0},{4,2},{6,4},{8,6},{10,8},{12,10},{14,12},{16,14},{18,... | collective-permute-start | bytes 98312 | tf_op jit(solution)/shard_map/ppermute | solution.py:47
  503.4 8.0 collective-permute-start.49
  511.4 8.3 collective-permute-start.51
  527.6 8.0 collective-permute-start.55
  535.6 8.4 collective-permute-start.57
  593.1 8.0 collective-permute-start.61
  595.0 14.4 %collective-permute-start.62 = (f32[64,128]{1,0:T(8,128)S(1)}, f32[64,128]{1,0:T(8,128)S(1)}, u32[]{:S(2)}, u32[]{:S(2)}) collective-permute-start(f32[64,128]{1,0:T(8,128)S(1)} %collective-permute-done.60), channel_id=1, source_target_pairs={{0,30},{2,0},{4,2},{6,4},{8,6},{10,8},{12,10},{14,12},{16,14},{18,... | collective-permute-start | bytes 98312 | tf_op jit(solution)/shard_map/ppermute | solution.py:47
  609.4 8.0 collective-permute-start.64
  617.4 8.0 collective-permute-start.66
  625.4 8.0 collective-permute-start.68
  633.4 8.0 collective-permute-start.70
  700.2 14.1 %collective-permute-start.77 = (f32[64,128]{1,0:T(8,128)S(1)}, f32[64,128]{1,0:T(8,128)S(1)}, u32[]{:S(2)}, u32[]{:S(2)}) collective-permute-start(f32[64,128]{1,0:T(8,128)S(1)} %collective-permute-done.75), channel_id=1, source_target_pairs={{0,30},{2,0},{4,2},{6,4},{8,6},{10,8},{12,10},{14,12},{16,14},{18,... | collective-permute-start | bytes 98312 | tf_op jit(solution)/shard_map/ppermute | solution.py:47
  722.3 8.0 collective-permute-start.81
  730.3 8.0 collective-permute-start.83
  746.3 8.1 collective-permute-start.87
  803.2 8.0 collective-permute-start.91
  805.2 14.2 %collective-permute-start.92 = (f32[64,128]{1,0:T(8,128)S(1)}, f32[64,128]{1,0:T(8,128)S(1)}, u32[]{:S(2)}, u32[]{:S(2)}) collective-permute-start(f32[64,128]{1,0:T(8,128)S(1)} %collective-permute-done.90), channel_id=1, source_target_pairs={{0,30},{2,0},{4,2},{6,4},{8,6},{10,8},{12,10},{14,12},{16,14},{18,... | collective-permute-start | bytes 98312 | tf_op jit(solution)/shard_map/ppermute | solution.py:47
  819.4 8.0 collective-permute-start.94
  827.4 8.0 collective-permute-start.96
  835.4 8.0 collective-permute-start.98
  843.3 13.6 %collective-permute-start.101 = (f32[64,128]{1,0:T(8,128)S(1)}, f32[64,128]{1,0:T(8,128)S(1)}, u32[]{:S(2)}, u32[]{:S(2)}) collective-permute-start(f32[64,128]{1,0:T(8,128)S(1)} %collective-permute-done.99), channel_id=1, source_target_pairs={{0,2},{2,4},{4,6},{6,8},{8,10},{10,12},{12,14},{14,16},{16,18},{18... | collective-permute-start | bytes 98312 | tf_op jit(solution)/shard_map/ppermute | solution.py:45
  850.6 14.4 %collective-permute-start.102 = (f32[64,128]{1,0:T(8,128)S(1)}, f32[64,128]{1,0:T(8,128)S(1)}, u32[]{:S(2)}, u32[]{:S(2)}) collective-permute-start(f32[64,128]{1,0:T(8,128)S(1)} %collective-permute-done.100), channel_id=1, source_target_pairs={{0,30},{2,0},{4,2},{6,4},{8,6},{10,8},{12,10},{14,12},{16,14},{18,... | collective-permute-start | bytes 98312 | tf_op jit(solution)/shard_map/ppermute | solution.py:47
  (65 other events, 2629.6 us)
Sparse Core Ops, SparseCore 0:
  59.7 18.0 all-reduce.2
